TPU v7x, 128 devices: a whole 4x4x4 slice. The times are simulated.
128 devices in a mesh: rows: 16 (over y, z), seq: 8 (over x, core).
Axes of the slice: x: 4, y: 4, z: 4, core: 2. Of those that a mesh axis runs over, the one named last changes fastest.
Arguments:
- residual_in: bfloat16 [16, 2048, 3200], P('rows', 'seq'), may hold values from -6 to 6
- norm_gain: float32 [3200], replicated, may hold values from 0.1 to 1.9
- qkv_weight: bfloat16 [3200, 6144], P(None, 'seq')
- qk_gain: float32 [2, 2048], P(None, 'seq')
- out_weight: bfloat16 [2048, 3200], P('seq'), may hold values from -0.125 to 0.125
- layer_scale: float32 [3200], replicated, may hold values from 1 to 6
- segment_ids: int32 [16, 2048], P('rows', 'seq'), may hold values from 0 to 2, as said below
- pad_mask: int32 [16, 2048], P('rows', 'seq'), may hold values from 0 to 1, as said below
- ln_weight: float32 [12800], replicated, may hold values from 0.1 to 1.9
- ln_bias: float32 [12800], replicated, may hold values from -3 to 3
- fc_weight: bfloat16 [12800, 6144], P('rows'), may hold values from -0.0546875 to 0.0546875
- fc_bias: float32 [6144], replicated, may hold values from -3 to 3
- owner: int32 [16], replicated, may hold values from 0 to 15, each once
Outputs:
- features: bfloat16 [16, 512, 6144], P('rows', 'seq')
Inputs may be any that keep to these rules, and one draw needn't show every extreme that they name: `segment_ids`: within a row, segment ids never fall and change only at multiples of 1024 tokens; picture tokens carry ids below 2, padding tokens carry 2 and stand at the end of the row; the first tile is never padding. pad_mask is 0 exactly where segment_ids equals 2. `owner`: each index of rows owns exactly one row.
All inputs are finite; a program needn't handle non-finite values.
Results may differ from a plain program's by a relative error of at most 0.025.
Values may be sent and summed in bfloat16 or wider, within the bound.
A program may use at most 128 MiB of HBM per device.

v0:
```python
import jax
import jax.numpy as jnp
from jax import lax
from jax.sharding import PartitionSpec as P

D = 3200
HEAD_DIM = 128
HEADS = 16
GRID = 32
MASK_SHIFT = 1000000.0


def attend_dense(query_norm, key_norm, value_half, row_segments, block_len, scale):
    length, heads_here = (query_norm.shape[0], query_norm.shape[1])
    block_count = length // block_len

    def one_block(packed):
        query_block, query_seg = packed
        scores = (
            jnp.einsum("qhd,khd->hqk", query_block, key_norm, preferred_element_type=jnp.float32)
            * scale
        )
        same_seg = (query_seg[:, None] == row_segments[None, :])[None]
        scores = jnp.where(same_seg, scores, -1e30)
        peak_val = jnp.max(scores, axis=-1, keepdims=True)
        exp_terms = jnp.exp(scores - peak_val)
        probs = (exp_terms / jnp.sum(exp_terms, axis=-1, keepdims=True)).astype(jnp.bfloat16)
        return jnp.einsum(
            "hqk,khd->qhd", probs, value_half, preferred_element_type=jnp.float32
        ).astype(jnp.bfloat16)

    blocks_out = lax.map(
        one_block,
        (
            query_norm.reshape(block_count, block_len, heads_here, HEAD_DIM),
            row_segments.reshape(block_count, block_len),
        ),
    )
    return blocks_out.reshape(length, heads_here * HEAD_DIM)


def per_device(
    residual_in,
    norm_gain,
    qkv_weight,
    qk_gain,
    out_weight,
    layer_scale,
    segment_ids,
    pad_mask,
    ln_weight,
    ln_bias,
    fc_weight,
    fc_bias,
    owner,
):
    seq_count = lax.axis_size("seq")
    seq_me = lax.axis_index("seq")
    tokens = residual_in[0].astype(jnp.float32)
    shard_rows = tokens.shape[0]
    normed = (
        tokens * lax.rsqrt(jnp.mean(tokens * tokens, axis=-1, keepdims=True) + 1e-06) * norm_gain
    ).astype(jnp.bfloat16)
    row_tokens = lax.all_gather(normed, "seq", axis=0, tiled=True)
    length = row_tokens.shape[0]
    heads_here = qkv_weight.shape[1] // (3 * HEAD_DIM)
    projected = jnp.dot(row_tokens, qkv_weight, preferred_element_type=jnp.float32).reshape(
        length, heads_here, 3, HEAD_DIM
    )
    query_raw = projected[:, :, 0]
    key_raw = projected[:, :, 1]
    value_half = projected[:, :, 2].astype(jnp.bfloat16)
    seg_spread = lax.dynamic_update_slice_in_dim(
        jnp.zeros((length,), jnp.float32),
        segment_ids[0].astype(jnp.float32),
        seq_me * shard_rows,
        0,
    )
    stats = lax.psum(
        jnp.stack(
            [
                jnp.sum(query_raw * query_raw, axis=(1, 2)),
                jnp.sum(key_raw * key_raw, axis=(1, 2)),
                seg_spread,
            ]
        ),
        "seq",
    )
    query_sq, key_sq, row_segments = (stats[0], stats[1], stats[2])
    norm_width = HEADS * HEAD_DIM
    gain_pair = qk_gain.reshape(2, heads_here, HEAD_DIM)
    query_norm = (
        query_raw * lax.rsqrt(query_sq / norm_width + 1e-06)[:, None, None] * gain_pair[0]
    ).astype(jnp.bfloat16)
    key_norm = (
        key_raw * lax.rsqrt(key_sq / norm_width + 1e-06)[:, None, None] * gain_pair[1]
    ).astype(jnp.bfloat16)
    block_len = min(512, length)
    scale = HEAD_DIM ** (-0.5)
    attended = attend_dense(query_norm, key_norm, value_half, row_segments, block_len, scale)
    group_width = attended.shape[1]
    own_heads = lax.all_to_all(attended.reshape(seq_count, shard_rows, group_width), "seq", 0, 0)
    full_out_weight = lax.all_gather(out_weight, "seq", axis=0, tiled=False)
    group_terms = jnp.einsum(
        "gtc,gcd->gtd", own_heads, full_out_weight, preferred_element_type=jnp.float32
    ).astype(jnp.bfloat16)
    attn = jnp.sum(group_terms.astype(jnp.float32), axis=0)
    hidden = tokens + layer_scale * attn
    half_grid = GRID // 2
    lines = shard_rows // (2 * GRID)
    merged_count = shard_rows // 4
    merged = jnp.transpose(hidden.reshape(lines, 2, half_grid, 2, D), (0, 2, 1, 3, 4)).reshape(
        merged_count, 4 * D
    )
    centre = merged - jnp.mean(merged, axis=-1, keepdims=True)
    spread = jnp.mean(centre * centre, axis=-1, keepdims=True)
    merged_norm = (centre * lax.rsqrt(spread + 1e-05) * ln_weight + ln_bias).astype(jnp.bfloat16)
    merged_mask = (
        pad_mask[0]
        .reshape(lines, 2, half_grid, 2)[:, 0, :, 0]
        .reshape(merged_count)
        .astype(jnp.float32)
    )
    row_count = lax.axis_size("rows")
    row_me = lax.axis_index("rows")
    slabs = lax.all_to_all(merged_norm, "rows", split_axis=1, concat_axis=0, tiled=True)
    owner_hot = (owner[None, :] == jnp.arange(row_count, dtype=jnp.int32)[:, None]).astype(
        jnp.bfloat16
    )
    ordered = jnp.einsum(
        "jp,pms->jms",
        owner_hot,
        slabs.reshape(row_count, merged_count, -1),
        preferred_element_type=jnp.float32,
    ).astype(jnp.bfloat16)
    ordered = ordered.reshape(row_count * merged_count, -1)
    partial = jnp.dot(ordered, fc_weight, preferred_element_type=jnp.float32).reshape(
        row_count, merged_count, -1
    )
    own_slot = (jnp.arange(row_count, dtype=jnp.int32) == owner[row_me]).astype(jnp.float32)
    shift = own_slot[:, None] * ((merged_mask - 1.0) * MASK_SHIFT)[None, :]
    partial = (partial + shift[:, :, None]).astype(jnp.bfloat16)
    summed = lax.psum_scatter(
        partial.reshape(row_count * merged_count, -1), "rows", scatter_dimension=0, tiled=True
    ).astype(jnp.float32)
    result = jax.nn.gelu(summed + fc_bias, approximate=False)
    return result.astype(jnp.bfloat16)[None]


def solution(mesh):
    return jax.shard_map(
        per_device,
        mesh=mesh,
        in_specs=(
            P("rows", "seq", None),
            P(),
            P(None, "seq"),
            P(None, "seq"),
            P("seq", None),
            P(),
            P("rows", "seq"),
            P("rows", "seq"),
            P(),
            P(),
            P("rows", None),
            P(),
            P(),
        ),
        out_specs=P("rows", "seq", None),
        check_vma=False,
    )
```

profile of v0, /device:TPU:1, one launch (start us, length us, event | category | flops | bytes accessed | tf_op | source)
XLA Modules:
  0.0 404.6 jit_solution(10836090393352335551)
XLA Ops:
  6.5 2.0 fusion.28
  8.5 2.4 fusion.30
  11.0 0.7 all-gather.6.cloned.1.call-update
  11.7 72.5 %all-gather.4.cloned.1.call-done = bf16[2048,3200]{1,0:T(8,128)(2,1)} async-done(((bf16[256,3200]{1,0:T(8,128)(2,1)}), bf16[2048,3200]{1,0:T(8,128)(2,1)}) %all-gather.4.cloned.1.call-update) | async-done | bytes 13107216 | tf_op jit(solution)/shard_map/all_gather | solution.py:64
  84.2 15.7 %fusion.74 = f32[2048,768]{0,1:T(8,128)S(1)} fusion(bf16[2048,3200]{1,0:T(8,128)(2,1)} %all-gather.4.cloned.1.call-done, bf16[3200,768]{1,0:T(8,128)(2,1)} %param.17), kind=kOutput, calls=%fused_computation.97 | convolution fusion | flops 10066329600 | bytes 24313856 | tf_op jit(solution)/shard_map/dot_general | solution.py:67
  100.1 2.5 fusion.72
  102.5 1.9 copy.44
  104.4 2.9 copy.43
  107.7 1.3 copy-done
  108.9 0.3 multiply_reduce_fusion.1
  109.3 22.6 %psum.7 = f32[3,2048]{1,0:T(4,128)S(1)} all-reduce(f32[3,2048]{1,0:T(4,128)S(1)} %pad_maximum_fusion), channel_id=1, replica_groups=mesh['rows'=16,'seq'=8] {'seq'}, use_global_device_ids=true, to_apply=%region_3.0 | all-reduce | flops 6144 | bytes 49152 | tf_op jit(solution)/shard_map/psum | solution.py:79
  132.0 1.3 copy.45
  133.3 3.0 multiply_convert_fusion
  136.3 1.3 fusion.33
  137.6 53.7 %while.10 = (s32[]{:T(128)}, bf16[4,512,2,128]{3,2,1,0:T(2,128)(2,1)S(1)}, f32[4,512]{1,0:T(4,128)S(1)}, f32[1,2048]{1,0:T(1,128)S(1)}, bf16[4,512,2,128]{3,1,0,...) while((s32[]{:T(128)}, ...), condition=%wide.region_7.8_spmd, body=%wide.region_4.7_spmd.sunk | while | flops 1087506432 | bytes 26237560 | solution.py:32
  137.6 0.7 broadcast_compare_fusion.2
  138.3 7.8 %fusion.90 = (f32[2,512]{1,0:T(2,128)S(1)}, f32[2,512,2048]{2,1,0:T(8,128)}) fusion(pred[512,2048]{1,0:T(8,128)(4,1)S(1)} %broadcast_compare_fusion.2, bf16[2048,2,128]{2,0,1:T(8,128)(2,1)} %get-tuple-element.158, bf16[4,512,2,128]{3,1,0,2:T(8,128)(2,1)} %get-tuple-element.157, s32[]{:T(128)} %get-tuple-element.145), kind=kOutput, calls=%fused_computation.94.clone.1 | convolution fusion | flops 545261568 | bytes 10752512 | tf_op jit(solution)/shard_map/while/body/eval_jaxpr/sub | solution.py:26
  146.1 4.7 %fusion.91 = bf16[1,512,2,128]{3,1,2,0:T(8,128)(2,1)S(1)} fusion(bf16[2048,2,128]{2,0,1:T(8,128)(2,1)S(1)} %copy-done.5, f32[2,512,2048]{2,1,0:T(8,128)} %get-tuple-element.135, f32[2,512]{1,0:T(2,128)S(1)} %get-tuple-element.136), kind=kOutput, calls=%fused_computation.11.clone.1 | convolution fusion | flops 541196288 | bytes 9703424 | tf_op jit(solution)/shard_map/while/body/eval_jaxpr/hqk,khd->qhd/dot_general | solution.py:28
  151.1 0.7 broadcast_compare_fusion.2
  151.8 7.7 %fusion.90 = (f32[2,512]{1,0:T(2,128)S(1)}, f32[2,512,2048]{2,1,0:T(8,128)}) fusion(pred[512,2048]{1,0:T(8,128)(4,1)S(1)} %broadcast_compare_fusion.2, bf16[2048,2,128]{2,0,1:T(8,128)(2,1)} %get-tuple-element.158, bf16[4,512,2,128]{3,1,0,2:T(8,128)(2,1)} %get-tuple-element.157, s32[]{:T(128)} %get-tuple-element.145), kind=kOutput, calls=%fused_computation.94.clone.1 | convolution fusion | flops 545261568 | bytes 10752512 | tf_op jit(solution)/shard_map/while/body/eval_jaxpr/sub | solution.py:26
  159.5 4.7 %fusion.91 = bf16[1,512,2,128]{3,1,2,0:T(8,128)(2,1)S(1)} fusion(bf16[2048,2,128]{2,0,1:T(8,128)(2,1)S(1)} %copy-done.5, f32[2,512,2048]{2,1,0:T(8,128)} %get-tuple-element.135, f32[2,512]{1,0:T(2,128)S(1)} %get-tuple-element.136), kind=kOutput, calls=%fused_computation.11.clone.1 | convolution fusion | flops 541196288 | bytes 9703424 | tf_op jit(solution)/shard_map/while/body/eval_jaxpr/hqk,khd->qhd/dot_general | solution.py:28
  164.5 0.7 broadcast_compare_fusion.2
  165.2 7.7 %fusion.90 = (f32[2,512]{1,0:T(2,128)S(1)}, f32[2,512,2048]{2,1,0:T(8,128)}) fusion(pred[512,2048]{1,0:T(8,128)(4,1)S(1)} %broadcast_compare_fusion.2, bf16[2048,2,128]{2,0,1:T(8,128)(2,1)} %get-tuple-element.158, bf16[4,512,2,128]{3,1,0,2:T(8,128)(2,1)} %get-tuple-element.157, s32[]{:T(128)} %get-tuple-element.145), kind=kOutput, calls=%fused_computation.94.clone.1 | convolution fusion | flops 545261568 | bytes 10752512 | tf_op jit(solution)/shard_map/while/body/eval_jaxpr/sub | solution.py:26
  172.9 4.7 %fusion.91 = bf16[1,512,2,128]{3,1,2,0:T(8,128)(2,1)S(1)} fusion(bf16[2048,2,128]{2,0,1:T(8,128)(2,1)S(1)} %copy-done.5, f32[2,512,2048]{2,1,0:T(8,128)} %get-tuple-element.135, f32[2,512]{1,0:T(2,128)S(1)} %get-tuple-element.136), kind=kOutput, calls=%fused_computation.11.clone.1 | convolution fusion | flops 541196288 | bytes 9703424 | tf_op jit(solution)/shard_map/while/body/eval_jaxpr/hqk,khd->qhd/dot_general | solution.py:28
  177.9 0.7 broadcast_compare_fusion.2
  178.6 7.7 %fusion.90 = (f32[2,512]{1,0:T(2,128)S(1)}, f32[2,512,2048]{2,1,0:T(8,128)}) fusion(pred[512,2048]{1,0:T(8,128)(4,1)S(1)} %broadcast_compare_fusion.2, bf16[2048,2,128]{2,0,1:T(8,128)(2,1)} %get-tuple-element.158, bf16[4,512,2,128]{3,1,0,2:T(8,128)(2,1)} %get-tuple-element.157, s32[]{:T(128)} %get-tuple-element.145), kind=kOutput, calls=%fused_computation.94.clone.1 | convolution fusion | flops 545261568 | bytes 10752512 | tf_op jit(solution)/shard_map/while/body/eval_jaxpr/sub | solution.py:26
  186.3 4.7 %fusion.91 = bf16[1,512,2,128]{3,1,2,0:T(8,128)(2,1)S(1)} fusion(bf16[2048,2,128]{2,0,1:T(8,128)(2,1)S(1)} %copy-done.5, f32[2,512,2048]{2,1,0:T(8,128)} %get-tuple-element.135, f32[2,512]{1,0:T(2,128)S(1)} %get-tuple-element.136), kind=kOutput, calls=%fused_computation.11.clone.1 | convolution fusion | flops 541196288 | bytes 9703424 | tf_op jit(solution)/shard_map/while/body/eval_jaxpr/hqk,khd->qhd/dot_general | solution.py:28
  191.3 1.5 reshape_reshape.3
  192.8 7.8 %all-to-all-start = ((bf16[8,256,256]{2,1,0:T(8,128)(2,1)}), bf16[8,256,256]{2,1,0:T(8,128)(2,1)S(1)}, u32[]{:S(2)}, u32[]{:S(2)}) async-start(bf16[8,256,256]{2,1,0:T(8,128)(2,1)} %reshape_reshape.3), calls=%async_computation | async-start | bytes 2097152 | tf_op jit(solution)/shard_map/all_to_all | solution.py:102
  200.6 2.8 reshape.214
  203.7 12.1 %all-to-all-done = bf16[8,256,256]{2,1,0:T(8,128)(2,1)S(1)} async-done(((bf16[8,256,256]{2,1,0:T(8,128)(2,1)}), bf16[8,256,256]{2,1,0:T(8,128)(2,1)S(1)}, u32[]{:S(2)}, u32[]{:S(2)}) %all-to-all-start) | async-done | bytes 1048608 | tf_op jit(solution)/shard_map/all_to_all | solution.py:102
  215.7 10.6 %convert_reduce_fusion = f32[256,3200]{1,0:T(8,128)} fusion(bf16[8,256,256]{2,1,0:T(8,128)(2,1)S(1)} %all-to-all-done, bf16[8,256,3200]{2,1,0:T(8,128)(2,1)} %bitcast.99), kind=kOutput, calls=%fused_computation.24 | convolution fusion | flops 3374284800 | bytes 17432576 | tf_op jit(solution)/shard_map/gtc,gcd->gtd/dot_general | solution.py:104
  226.3 5.3 %reduce_sum.69 = f32[4,2,16,2,3200]{4,3,2,1,0:T(2,128)} reshape(f32[256,3200]{1,0:T(8,128)} %convert_reduce_fusion) | data formatting | bytes 6553600 | tf_op jit(solution)/shard_map/reduce_sum | solution.py:107
  231.7 4.2 %fusion.66 = (f32[4,16]{1,0:T(4,128)S(1)}, f32[4,16,2,2,3200]{4,3,1,2,0:T(2,128)S(1)}) fusion(f32[4,2,16,2,3200]{4,3,2,1,0:T(2,128)S(1)} %copy-done.3, f32[4,2,16,2,3200]{4,3,2,1,0:T(2,128)} %reduce_sum.69, f32[3200]{0:T(1024)S(1)} %copy-done.9), kind=kLoop, calls=%fused_computation.93 | loop fusion | flops 2457536 | bytes 9843456 | tf_op jit(solution)/shard_map/reduce_sum | solution.py:115
  236.2 1.9 multiply_reduce_fusion
  238.3 4.5 %reshape.212 = f32[64,16,800]{2,1,0:T(8,128)} reshape(f32[4,16,2,2,3200]{4,3,2,1,0:T(2,128)S(1)} %copy.36) | data formatting | bytes 6553600 | tf_op jit(solution)/shard_map/reshape | solution.py:112
  242.7 2.7 add_convert_fusion.1
  245.5 1.7 copy.37
  247.1 7.0 %all-to-all-start.1 = ((bf16[64,16,800]{2,0,1:T(8,128)(2,1)}), bf16[64,16,800]{2,0,1:T(8,128)(2,1)S(1)}, u32[]{:S(2)}, u32[]{:S(2)}) async-start(bf16[64,16,800]{2,0,1:T(8,128)(2,1)} %copy.37), calls=%async_computation.1 | async-start | bytes 3670016 | tf_op jit(solution)/shard_map/all_to_all | solution.py:126
  254.2 0.5 broadcast.188
  254.7 0.7 reduce.16
  255.7 0.6 dynamic_slice.11
  256.3 0.6 compare_convert_fusion
  257.0 20.2 %all-to-all-done.1 = bf16[64,16,800]{2,0,1:T(8,128)(2,1)S(1)} async-done(((bf16[64,16,800]{2,0,1:T(8,128)(2,1)}), bf16[64,16,800]{2,0,1:T(8,128)(2,1)S(1)}, u32[]{:S(2)}, u32[]{:S(2)}) %all-to-all-start.1) | async-done | bytes 1638432 | tf_op jit(solution)/shard_map/all_to_all | solution.py:126
  277.2 1.3 fusion.38
  278.5 19.2 %add_convert_fusion = bf16[16,64,6144]{2,1,0:T(8,128)(2,1)} fusion(f32[16,64]{1,0:T(8,128)S(1)} %broadcast_multiply_fusion, bf16[800,6144]{1,0:T(8,128)(2,1)} %param.25, bf16[16,64,800]{2,0,1:T(8,128)(2,1)S(1)} %fusion.38), kind=kOutput, calls=%fused_computation.25 | convolution fusion | flops 10078912512 | bytes 24055808 | tf_op jit(solution)/shard_map/dot_general | solution.py:137
  297.8 95.1 %reduce-scatter.2.cloned.1.call-done = bf16[64,6144]{1,0:T(8,128)(2,1)} async-done(((bf16[1024,6144]{1,0:T(8,128)(2,1)}), bf16[64,6144]{1,0:T(8,128)(2,1)}) %reduce-scatter.2.cloned.1.call-update) | async-done | bytes 786448 | tf_op jit(solution)/shard_map/reduce_scatter | solution.py:143
  392.9 5.2 %fusion.54 = bf16[1,64,6144]{2,1,0:T(8,128)(2,1)} fusion(bf16[64,6144]{1,0:T(8,128)(2,1)} %reduce-scatter.2.cloned.1.call-done, f32[6144]{0:T(1024)S(1)} %copy-done.8), kind=kLoop, calls=%fused_computation.70 | loop fusion | flops 26345472 | bytes 1597440 | tf_op jit(solution)/shard_map/broadcast_in_dim | solution.py:147
  (69 shorter events, 3.1 us)
Async XLA Ops:
  6.5 2.0 copy-start.1
  6.5 77.7 %all-gather.4.cloned.1.call-start = ((), (), s32[]{:S(2)}) async-start(), calls=%async_computation.3 | async-start | bytes 14745600 | tf_op jit(solution)/shard_map/all_gather | solution.py:64
  10.9 0.8 copy-start.11
  10.9 0.8 copy-start.10
  10.9 192.8 %all-gather.6.cloned.1.call-start = ((), (), s32[]{:S(2)}) async-start(), calls=%async_computation.5 | async-start | bytes 14745600 | tf_op jit(solution)/shard_map/all_gather | solution.py:103
  107.3 1.6 copy-start
  136.3 1.3 copy-start.4
  138.3 7.8 %copy-start.5 = (bf16[2048,2,128]{2,0,1:T(8,128)(2,1)S(1)}, bf16[2048,2,128]{2,0,1:T(8,128)(2,1)}, u32[]{:S(2)}) copy-start(bf16[2048,2,128]{2,0,1:T(8,128)(2,1)} %get-tuple-element.159) | copy-start | bytes 3145732 | tf_op jit(solution)/shard_map/while
  151.7 7.8 %copy-start.5 = (bf16[2048,2,128]{2,0,1:T(8,128)(2,1)S(1)}, bf16[2048,2,128]{2,0,1:T(8,128)(2,1)}, u32[]{:S(2)}) copy-start(bf16[2048,2,128]{2,0,1:T(8,128)(2,1)} %get-tuple-element.159) | copy-start | bytes 3145732 | tf_op jit(solution)/shard_map/while
  165.2 7.8 %copy-start.5 = (bf16[2048,2,128]{2,0,1:T(8,128)(2,1)S(1)}, bf16[2048,2,128]{2,0,1:T(8,128)(2,1)}, u32[]{:S(2)}) copy-start(bf16[2048,2,128]{2,0,1:T(8,128)(2,1)} %get-tuple-element.159) | copy-start | bytes 3145732 | tf_op jit(solution)/shard_map/while
  178.6 7.8 %copy-start.5 = (bf16[2048,2,128]{2,0,1:T(8,128)(2,1)S(1)}, bf16[2048,2,128]{2,0,1:T(8,128)(2,1)}, u32[]{:S(2)}) copy-start(bf16[2048,2,128]{2,0,1:T(8,128)(2,1)} %get-tuple-element.159) | copy-start | bytes 3145732 | tf_op jit(solution)/shard_map/while
  191.3 9.3 %copy-start.2 = (bf16[1,256,3200]{2,1,0:T(8,128)(2,1)S(1)}, bf16[1,256,3200]{2,1,0:T(8,128)(2,1)}, u32[]{:S(2)}) copy-start(bf16[1,256,3200]{2,1,0:T(8,128)(2,1)} %param.15) | copy-start | bytes 4915204
  192.8 22.9 %all-to-all-start = ((bf16[8,256,256]{2,1,0:T(8,128)(2,1)}), bf16[8,256,256]{2,1,0:T(8,128)(2,1)S(1)}, u32[]{:S(2)}, u32[]{:S(2)}) async-start(bf16[8,256,256]{2,1,0:T(8,128)(2,1)} %reshape_reshape.3), calls=%async_computation | async-start | bytes 2097152 | tf_op jit(solution)/shard_map/all_to_all | solution.py:102
  200.6 2.8 copy-start.6
  200.6 2.9 copy-start.7
  226.3 5.3 %copy-start.3 = (f32[4,2,16,2,3200]{4,3,2,1,0:T(2,128)S(1)}, f32[4,2,16,2,3200]{4,3,2,1,0:T(2,128)}, u32[]{:S(2)}) copy-start(f32[4,2,16,2,3200]{4,3,2,1,0:T(2,128)} %reshape.214) | copy-start | bytes 9830404
  226.3 5.3 %copy-start.9 = (f32[3200]{0:T(1024)S(1)}, f32[3200]{0:T(1024)}, u32[]{:S(2)}) copy-start(f32[3200]{0:T(1024)} %param.20) | copy-start | bytes 38404
  247.1 7.6 %copy-start.12 = (s32[1,256]{1,0:T(1,128)S(1)}, s32[1,256]{1,0:T(1,128)}, u32[]{:S(2)}) copy-start(s32[1,256]{1,0:T(1,128)} %param.22) | copy-start | bytes 3076
  247.1 8.6 %copy-start.13 = (s32[16]{0:T(128)S(1)}, s32[16]{0:T(128)}, u32[]{:S(2)}) copy-start(s32[16]{0:T(128)} %param.27) | copy-start | bytes 196
  247.1 30.1 %all-to-all-start.1 = ((bf16[64,16,800]{2,0,1:T(8,128)(2,1)}), bf16[64,16,800]{2,0,1:T(8,128)(2,1)S(1)}, u32[]{:S(2)}, u32[]{:S(2)}) async-start(bf16[64,16,800]{2,0,1:T(8,128)(2,1)} %copy.37), calls=%async_computation.1 | async-start | bytes 3670016 | tf_op jit(solution)/shard_map/all_to_all | solution.py:126
  254.2 138.7 %reduce-scatter.2.cloned.1.call-start = ((), (), s32[]{:S(2)}) async-start(), calls=%async_computation.4 | async-start | bytes 13369344 | tf_op jit(solution)/shard_map/reduce_scatter | solution.py:143
  297.7 95.1 %copy-start.8 = (f32[6144]{0:T(1024)S(1)}, f32[6144]{0:T(1024)}, u32[]{:S(2)}) copy-start(f32[6144]{0:T(1024)} %param.26) | copy-start | bytes 73732
Sparse Core Ops, SparseCore 0:
  11.0 73.1 all-gather.3
  85.9 70.2 all-gather.5
  297.9 94.9 reduce-scatter.1
where the time goes:
time: 405 us
  waiting for transfers between devices  201 us (50%)
  matrix products  96.5 us (24%)
  local copies, waits for them, and re-layouts  29 us (7%)
  other arithmetic  27.6 us (7%)
  blocking collectives  22.6 us (6%)
  starting transfers between devices  14.9 us (4%)
  between operations  13.3 us (3%)
    reduce_scatter x1, waiting for transfers between devices, per_device(): lax.psum_scatter(partial.reshape(row_count * merged_count, -1), 'rows', s...  95.1 us
    all_gather x1, waiting for transfers between devices, per_device(): row_tokens = lax.all_gather(normed, 'seq', axis=0, tiled=True)  72.5 us
    sub x4, matrix products, one_block(): exp_terms = jnp.exp(scores - peak_val)  31 us
    psum x1, blocking collectives, per_device(): lax.psum(jnp.stack([jnp.sum(query_raw * query_raw, axis=(1, 2)), jnp.sum(...  22.6 us
    all_to_all x1, waiting for transfers between devices, per_device(): lax.all_to_all(merged_norm, 'rows', split_axis=1, concat_axis=0, tiled=True)  20.2 us
    dot_general x1, matrix products, per_device(): jnp.dot(ordered, fc_weight, preferred_element_type=jnp.float32)  19.2 us
    dot_general x4, matrix products, one_block(): jnp.einsum('hqk,khd->qhd', probs, value_half, preferred_element_type=jnp....  18.7 us
    dot_general x1, matrix products, per_device(): jnp.dot(row_tokens, qkv_weight, preferred_element_type=jnp.float32)  15.7 us
  transfers between devices with their start and end apart: 5, of which 4 were waited for; matrix products, arithmetic and copies ran while one was open for 22% of the time, Pallas kernels for 0%

commit v1 on v0

--- a/solution.py
+++ b/solution.py
@@ -8,6 +8,27 @@
 HEADS = 16
 GRID = 32
 MASK_SHIFT = 1000000.0
+
+
+def collect(x, axis, dim):
+    size, place, rows = (lax.axis_size(axis), lax.axis_index(axis), x.shape[dim])
+    right = [(i, (i + 1) % size) for i in range(size)]
+    downward = [(i, (i - 1) % size) for i in range(size)]
+    out = jnp.zeros((*x.shape[:dim], size * rows, *x.shape[dim + 1 :]), x.dtype)
+    out = lax.dynamic_update_slice_in_dim(out, x, place * rows, axis=dim)
+    from_left = from_right = x
+    halfway = size // 2
+    for step in range(1, halfway + 1):
+        from_left = lax.ppermute(from_left, axis, right)
+        out = lax.dynamic_update_slice_in_dim(
+            out, from_left, (place - step) % size * rows, axis=dim
+        )
+        if step < size - halfway:
+            from_right = lax.ppermute(from_right, axis, downward)
+            out = lax.dynamic_update_slice_in_dim(
+                out, from_right, (place + step) % size * rows, axis=dim
+            )
+    return out
 
 
 def attend_dense(query_norm, key_norm, value_half, row_segments, block_len, scale):
@@ -61,7 +82,7 @@
     normed = (
         tokens * lax.rsqrt(jnp.mean(tokens * tokens, axis=-1, keepdims=True) + 1e-06) * norm_gain
     ).astype(jnp.bfloat16)
-    row_tokens = lax.all_gather(normed, "seq", axis=0, tiled=True)
+    row_tokens = collect(normed, "seq", 0)
     length = row_tokens.shape[0]
     heads_here = qkv_weight.shape[1] // (3 * HEAD_DIM)
     projected = jnp.dot(row_tokens, qkv_weight, preferred_element_type=jnp.float32).reshape(

time: 405 us -> 470 us (1.16)
  waiting for transfers between devices: 201 us -> 231 us
  local copies, waits for them, and re-layouts: 29 us -> 48 us
  starting transfers between devices: 14.9 us -> 28.5 us
    ppermute x0 -> x7, waiting for transfers between devices: none -> 104 us  [the longest x4 104 us: collect(): from_left = lax.ppermute(from_left, axis, right)]
    all_gather x1 -> x0, waiting for transfers between devices: 72.5 us -> none  [per_device(): row_tokens = lax.all_gather(normed, 'seq', axis=0, tiled=True)]
    dynamic_update_slice x0 -> x7, local copies, waits for them, and re-layouts: none -> 13.4 us  [the longest x4 8.1 us: collect(): lax.dynamic_update_slice_in_dim(out, from_left, (place - step) % size * r...]
    ppermute x0 -> x7, starting transfers between devices: none -> 13 us  [the longest x4 10 us: collect(): from_left = lax.ppermute(from_left, axis, right)]
    broadcast_in_dim x0 -> x1, local copies, waits for them, and re-layouts: none -> 5.6 us  [collect(): out = jnp.zeros((*x.shape[:dim], size * rows, *x.shape[dim + 1:]), x.dtype)]
  transfers between devices with their start and end apart: 5 -> 11, of which waited for: 4 -> 7; matrix products, arithmetic and copies ran while one was open for 22% -> 22% of each run, Pallas kernels for 0% -> 0%
where the time goes in v1:
time: 470 us; the launch traced here: 469 us
  waiting for transfers between devices  231 us (49%)
  matrix products  96.4 us (21%)
  local copies, waits for them, and re-layouts  48 us (10%)
  starting transfers between devices  28.5 us (6%)
  other arithmetic  26.7 us (6%)
  blocking collectives  23.9 us (5%)
  between operations  13.6 us (3%)
    ppermute x4, waiting for transfers between devices, collect(): from_left = lax.ppermute(from_left, axis, right)  104 us
    reduce_scatter x1, waiting for transfers between devices, per_device(): lax.psum_scatter(partial.reshape(row_count * merged_count, -1), 'rows', s...  95.1 us
    sub x4, matrix products, one_block(): exp_terms = jnp.exp(scores - peak_val)  31 us
    psum x1, blocking collectives, per_device(): lax.psum(jnp.stack([jnp.sum(query_raw * query_raw, axis=(1, 2)), jnp.sum(...  23.9 us
    all_to_all x1, waiting for transfers between devices, per_device(): lax.all_to_all(merged_norm, 'rows', split_axis=1, concat_axis=0, tiled=True)  20.2 us
    dot_general x1, matrix products, per_device(): jnp.dot(ordered, fc_weight, preferred_element_type=jnp.float32)  19.2 us
    dot_general x4, matrix products, one_block(): jnp.einsum('hqk,khd->qhd', probs, value_half, preferred_element_type=jnp....  18.7 us
    dot_general x1, matrix products, per_device(): jnp.dot(row_tokens, qkv_weight, preferred_element_type=jnp.float32)  15.7 us
  transfers between devices with their start and end apart: 11, of which 7 were waited for; matrix products, arithmetic and copies ran while one was open for 22% of the time, Pallas kernels for 0%

profile of v1, /device:TPU:1, one launch (start us, length us, event | category | flops | bytes accessed | tf_op | source)
XLA Modules:
  0.0 468.6 jit_solution(11617377997142770810)
XLA Ops:
  6.5 1.8 fusion.28
  8.4 5.6 %broadcast_in_dim.29 = bf16[2048,3200]{1,0:T(8,128)(2,1)} broadcast(bf16[]{:T(256)} %constant.58.clone.1), dimensions={} | broadcast | bytes 13107202 | tf_op jit(solution)/shard_map/broadcast_in_dim | solution.py:17
  14.0 1.7 constant_dynamic-update-slice_fusion.8
  15.7 2.6 collective-permute-start
  18.3 27.1 %collective-permute-done = bf16[256,3200]{1,0:T(8,128)(2,1)S(1)} collective-permute-done((bf16[256,3200]{1,0:T(8,128)(2,1)S(1)}, bf16[256,3200]{1,0:T(8,128)(2,1)S(1)}, u32[]{:S(2)}, u32[]{:S(2)}) %collective-permute-start) | collective-permute-done | bytes 1638432 | tf_op jit(solution)/shard_map/ppermute | solution.py:22
  45.4 2.5 collective-permute-start.2
  47.9 2.0 collective-permute-start.3
  49.8 51.2 %collective-permute-done.2 = bf16[256,3200]{1,0:T(8,128)(2,1)} collective-permute-done((bf16[256,3200]{1,0:T(8,128)(2,1)S(1)}, bf16[256,3200]{1,0:T(8,128)(2,1)}, u32[]{:S(2)}, u32[]{:S(2)}) %collective-permute-start.2) | collective-permute-done | bytes 1638432 | tf_op jit(solution)/shard_map/ppermute | solution.py:22
  101.0 2.6 collective-permute-start.4
  103.6 2.7 constant_dynamic-update-slice_fusion.7
  107.4 2.7 constant_dynamic-update-slice_fusion.6
  110.1 14.1 %collective-permute-done.4 = bf16[256,3200]{1,0:T(8,128)(2,1)S(1)} collective-permute-done((bf16[256,3200]{1,0:T(8,128)(2,1)}, bf16[256,3200]{1,0:T(8,128)(2,1)S(1)}, u32[]{:S(2)}, u32[]{:S(2)}) %collective-permute-start.4) | collective-permute-done | bytes 1638432 | tf_op jit(solution)/shard_map/ppermute | solution.py:22
  124.2 2.4 collective-permute-start.6
  126.6 2.8 constant_dynamic-update-slice_fusion.5
  133.2 11.4 %collective-permute-done.6 = bf16[256,3200]{1,0:T(8,128)(2,1)S(1)} collective-permute-done((bf16[256,3200]{1,0:T(8,128)(2,1)S(1)}, bf16[256,3200]{1,0:T(8,128)(2,1)S(1)}, u32[]{:S(2)}, u32[]{:S(2)}) %collective-permute-start.6) | collective-permute-done | bytes 1638432 | tf_op jit(solution)/shard_map/ppermute | solution.py:22
  144.6 1.3 constant_dynamic-update-slice_fusion.1
  146.0 15.7 %fusion.75 = f32[2048,768]{0,1:T(8,128)S(1)} fusion(bf16[2048,3200]{1,0:T(8,128)(2,1)} %constant_dynamic-update-slice_fusion.1, bf16[3200,768]{1,0:T(8,128)(2,1)} %param.17), kind=kOutput, calls=%fused_computation.105 | convolution fusion | flops 10066329600 | bytes 24313856 | tf_op jit(solution)/shard_map/dot_general | solution.py:88
  161.8 2.5 fusion.73
  164.3 1.9 copy.44
  166.2 2.9 copy.43
  171.0 23.9 %psum.7 = f32[3,2048]{1,0:T(4,128)S(1)} all-reduce(f32[3,2048]{1,0:T(4,128)S(1)} %pad_maximum_fusion), channel_id=1, replica_groups=mesh['rows'=16,'seq'=8] {'seq'}, use_global_device_ids=true, to_apply=%region_3.4 | all-reduce | flops 6144 | bytes 49152 | tf_op jit(solution)/shard_map/psum | solution.py:100
  195.1 1.3 copy.45
  196.4 3.0 multiply_convert_fusion
  200.7 53.7 %while.10 = (s32[]{:T(128)}, bf16[4,512,2,128]{3,2,1,0:T(2,128)(2,1)S(1)}, f32[4,512]{1,0:T(4,128)S(1)}, f32[1,2048]{1,0:T(1,128)S(1)}, bf16[4,512,2,128]{3,1,0,...) while((s32[]{:T(128)}, ...), condition=%wide.region_7.8_spmd, body=%wide.region_4.7_spmd.sunk | while | flops 1087506432 | bytes 26237560 | solution.py:53
  201.3 7.7 %fusion.91 = (f32[2,512]{1,0:T(2,128)S(1)}, f32[2,512,2048]{2,1,0:T(8,128)}) fusion(pred[512,2048]{1,0:T(8,128)(4,1)S(1)} %broadcast_compare_fusion.2, bf16[2048,2,128]{2,0,1:T(8,128)(2,1)} %get-tuple-element.160, bf16[4,512,2,128]{3,1,0,2:T(8,128)(2,1)} %get-tuple-element.159, s32[]{:T(128)} %get-tuple-element.147), kind=kOutput, calls=%fused_computation.102.clone.1 | convolution fusion | flops 545261568 | bytes 10752512 | tf_op jit(solution)/shard_map/while/body/eval_jaxpr/sub | solution.py:47
  209.1 4.7 fusion.92
  214.8 7.7 %fusion.91 = (f32[2,512]{1,0:T(2,128)S(1)}, f32[2,512,2048]{2,1,0:T(8,128)}) fusion(pred[512,2048]{1,0:T(8,128)(4,1)S(1)} %broadcast_compare_fusion.2, bf16[2048,2,128]{2,0,1:T(8,128)(2,1)} %get-tuple-element.160, bf16[4,512,2,128]{3,1,0,2:T(8,128)(2,1)} %get-tuple-element.159, s32[]{:T(128)} %get-tuple-element.147), kind=kOutput, calls=%fused_computation.102.clone.1 | convolution fusion | flops 545261568 | bytes 10752512 | tf_op jit(solution)/shard_map/while/body/eval_jaxpr/sub | solution.py:47
  222.5 4.7 fusion.92
  228.2 7.7 %fusion.91 = (f32[2,512]{1,0:T(2,128)S(1)}, f32[2,512,2048]{2,1,0:T(8,128)}) fusion(pred[512,2048]{1,0:T(8,128)(4,1)S(1)} %broadcast_compare_fusion.2, bf16[2048,2,128]{2,0,1:T(8,128)(2,1)} %get-tuple-element.160, bf16[4,512,2,128]{3,1,0,2:T(8,128)(2,1)} %get-tuple-element.159, s32[]{:T(128)} %get-tuple-element.147), kind=kOutput, calls=%fused_computation.102.clone.1 | convolution fusion | flops 545261568 | bytes 10752512 | tf_op jit(solution)/shard_map/while/body/eval_jaxpr/sub | solution.py:47
  235.9 4.7 fusion.92
  241.6 7.7 %fusion.91 = (f32[2,512]{1,0:T(2,128)S(1)}, f32[2,512,2048]{2,1,0:T(8,128)}) fusion(pred[512,2048]{1,0:T(8,128)(4,1)S(1)} %broadcast_compare_fusion.2, bf16[2048,2,128]{2,0,1:T(8,128)(2,1)} %get-tuple-element.160, bf16[4,512,2,128]{3,1,0,2:T(8,128)(2,1)} %get-tuple-element.159, s32[]{:T(128)} %get-tuple-element.147), kind=kOutput, calls=%fused_computation.102.clone.1 | convolution fusion | flops 545261568 | bytes 10752512 | tf_op jit(solution)/shard_map/while/body/eval_jaxpr/sub | solution.py:47
  249.3 4.7 fusion.92
  254.3 1.5 reshape_reshape.3
  255.8 7.0 %all-to-all-start = ((bf16[8,256,256]{2,1,0:T(8,128)(2,1)}), bf16[8,256,256]{2,1,0:T(8,128)(2,1)S(1)}, u32[]{:S(2)}, u32[]{:S(2)}) async-start(bf16[8,256,256]{2,1,0:T(8,128)(2,1)} %reshape_reshape.3), calls=%async_computation | async-start | bytes 2097152 | tf_op jit(solution)/shard_map/all_to_all | solution.py:123
  262.9 2.8 reshape.214
  265.9 12.1 %all-to-all-done = bf16[8,256,256]{2,1,0:T(8,128)(2,1)S(1)} async-done(((bf16[8,256,256]{2,1,0:T(8,128)(2,1)}), bf16[8,256,256]{2,1,0:T(8,128)(2,1)S(1)}, u32[]{:S(2)}, u32[]{:S(2)}) %all-to-all-start) | async-done | bytes 1048608 | tf_op jit(solution)/shard_map/all_to_all | solution.py:123
  278.0 10.6 %convert_reduce_fusion = f32[256,3200]{1,0:T(8,128)} fusion(bf16[8,256,256]{2,1,0:T(8,128)(2,1)S(1)} %all-to-all-done, bf16[8,256,3200]{2,1,0:T(8,128)(2,1)} %bitcast.100), kind=kOutput, calls=%fused_computation.24 | convolution fusion | flops 3374284800 | bytes 17432576 | tf_op jit(solution)/shard_map/gtc,gcd->gtd/dot_general | solution.py:125
  288.5 5.3 %reduce_sum.69 = f32[4,2,16,2,3200]{4,3,2,1,0:T(2,128)} reshape(f32[256,3200]{1,0:T(8,128)} %convert_reduce_fusion) | data formatting | bytes 6553600 | tf_op jit(solution)/shard_map/reduce_sum | solution.py:128
  293.9 4.2 fusion.66
  298.4 1.9 multiply_reduce_fusion
  300.5 4.5 reshape.212
  305.0 2.7 add_convert_fusion.1
  307.7 1.7 copy.37
  309.4 8.4 %all-to-all-start.1 = ((bf16[64,16,800]{2,0,1:T(8,128)(2,1)}), bf16[64,16,800]{2,0,1:T(8,128)(2,1)S(1)}, u32[]{:S(2)}, u32[]{:S(2)}) async-start(bf16[64,16,800]{2,0,1:T(8,128)(2,1)} %copy.37), calls=%async_computation.1 | async-start | bytes 3670016 | tf_op jit(solution)/shard_map/all_to_all | solution.py:147
  320.7 20.2 %all-to-all-done.1 = bf16[64,16,800]{2,0,1:T(8,128)(2,1)S(1)} async-done(((bf16[64,16,800]{2,0,1:T(8,128)(2,1)}), bf16[64,16,800]{2,0,1:T(8,128)(2,1)S(1)}, u32[]{:S(2)}, u32[]{:S(2)}) %all-to-all-start.1) | async-done | bytes 1638432 | tf_op jit(solution)/shard_map/all_to_all | solution.py:147
  342.1 19.2 %add_convert_fusion = bf16[16,64,6144]{2,1,0:T(8,128)(2,1)} fusion(f32[16,64]{1,0:T(8,128)S(1)} %broadcast_multiply_fusion, bf16[800,6144]{1,0:T(8,128)(2,1)} %param.25, bf16[16,64,800]{2,0,1:T(8,128)(2,1)S(1)} %fusion.38), kind=kOutput, calls=%fused_computation.25 | convolution fusion | flops 10078912512 | bytes 24055808 | tf_op jit(solution)/shard_map/dot_general | solution.py:158
  361.4 95.1 %reduce-scatter.2.cloned.1.call-done = bf16[64,6144]{1,0:T(8,128)(2,1)} async-done(((bf16[1024,6144]{1,0:T(8,128)(2,1)}), bf16[64,6144]{1,0:T(8,128)(2,1)}) %reduce-scatter.2.cloned.1.call-update) | async-done | bytes 786448 | tf_op jit(solution)/shard_map/reduce_scatter | solution.py:164
  456.5 5.2 %fusion.54 = bf16[1,64,6144]{2,1,0:T(8,128)(2,1)} fusion(bf16[64,6144]{1,0:T(8,128)(2,1)} %reduce-scatter.2.cloned.1.call-done, f32[6144]{0:T(1024)S(1)} %copy-done.9), kind=kLoop, calls=%fused_computation.70 | loop fusion | flops 26345472 | bytes 1597440 | tf_op jit(solution)/shard_map/broadcast_in_dim | solution.py:168
  (92 shorter events, 17.1 us)
Async XLA Ops:
  6.5 271.4 %all-gather.3.cloned.1.call-start = ((), (), s32[]{:S(2)}) async-start(), calls=%async_computation.4 | async-start | bytes 14745600 | tf_op jit(solution)/shard_map/all_gather | solution.py:124
  8.4 5.6 %copy-start.1 = (bf16[1,256,3200]{2,1,0:T(8,128)(2,1)S(1)}, bf16[1,256,3200]{2,1,0:T(8,128)(2,1)}, u32[]{:S(2)}) copy-start(bf16[1,256,3200]{2,1,0:T(8,128)(2,1)} %param.15) | copy-start | bytes 4915204
  8.4 5.6 %copy-start.10 = (f32[3200]{0:T(1024)S(1)}, f32[3200]{0:T(1024)}, u32[]{:S(2)}) copy-start(f32[3200]{0:T(1024)} %param.16) | copy-start | bytes 38404
  15.7 87.9 %copy-start.13 = (s32[1,256]{1,0:T(1,128)S(1)}, s32[1,256]{1,0:T(1,128)}, u32[]{:S(2)}) copy-start(s32[1,256]{1,0:T(1,128)} %param.21) | copy-start | bytes 3076
  15.7 88.0 %copy-start.12 = (f32[2,256]{1,0:T(2,128)S(1)}, f32[2,256]{1,0:T(2,128)}, u32[]{:S(2)}) copy-start(f32[2,256]{1,0:T(2,128)} %param.18) | copy-start | bytes 6148
  15.7 29.7 %collective-permute-start = (bf16[256,3200]{1,0:T(8,128)(2,1)S(1)}, bf16[256,3200]{1,0:T(8,128)(2,1)S(1)}, u32[]{:S(2)}, u32[]{:S(2)}) collective-permute-start(bf16[256,3200]{1,0:T(8,128)(2,1)S(1)} %get-tuple-element.83), channel_id=1, source_target_pairs={{0,1},{1,2},{2,3},{3,4},{4,5},{5,6},{6,7},{7,0},{8,9},{9,10},{10,1... | collective-permute-start | bytes 4915208 | tf_op jit(solution)/shard_map/ppermute | solution.py:22
  18.3 29.6 %collective-permute-start.1 = (bf16[256,3200]{1,0:T(8,128)(2,1)S(1)}, bf16[256,3200]{1,0:T(8,128)(2,1)}, u32[]{:S(2)}, u32[]{:S(2)}) collective-permute-start(bf16[256,3200]{1,0:T(8,128)(2,1)S(1)} %get-tuple-element.83), channel_id=1, source_target_pairs={{0,7},{1,0},{2,1},{3,2},{4,3},{5,4},{6,5},{7,6},{8,15},{9,8},{10,9... | collective-permute-start | bytes 4915208 | tf_op jit(solution)/shard_map/ppermute | solution.py:27
  45.4 4.4 copy-start.4
  45.4 55.6 %collective-permute-start.2 = (bf16[256,3200]{1,0:T(8,128)(2,1)S(1)}, bf16[256,3200]{1,0:T(8,128)(2,1)}, u32[]{:S(2)}, u32[]{:S(2)}) collective-permute-start(bf16[256,3200]{1,0:T(8,128)(2,1)S(1)} %collective-permute-done), channel_id=1, source_target_pairs={{0,1},{1,2},{2,3},{3,4},{4,5},{5,6},{6,7},{7,0},{8,9},{9,10},{10,1... | collective-permute-start | bytes 4915208 | tf_op jit(solution)/shard_map/ppermute | solution.py:22
  47.9 58.5 %collective-permute-start.3 = (bf16[256,3200]{1,0:T(8,128)(2,1)}, bf16[256,3200]{1,0:T(8,128)(2,1)S(1)}, u32[]{:S(2)}, u32[]{:S(2)}) collective-permute-start(bf16[256,3200]{1,0:T(8,128)(2,1)} %collective-permute-done.1), channel_id=1, source_target_pairs={{0,7},{1,0},{2,1},{3,2},{4,3},{5,4},{6,5},{7,6},{8,15},{9,8},{10,9... | collective-permute-start | bytes 4915208 | tf_op jit(solution)/shard_map/ppermute | solution.py:27
  101.0 23.2 %collective-permute-start.4 = (bf16[256,3200]{1,0:T(8,128)(2,1)}, bf16[256,3200]{1,0:T(8,128)(2,1)S(1)}, u32[]{:S(2)}, u32[]{:S(2)}) collective-permute-start(bf16[256,3200]{1,0:T(8,128)(2,1)} %collective-permute-done.2), channel_id=1, source_target_pairs={{0,1},{1,2},{2,3},{3,4},{4,5},{5,6},{6,7},{7,0},{8,9},{9,10},{10,1... | collective-permute-start | bytes 4915208 | tf_op jit(solution)/shard_map/ppermute | solution.py:22
  106.4 25.6 %collective-permute-start.5 = (bf16[256,3200]{1,0:T(8,128)(2,1)S(1)}, bf16[256,3200]{1,0:T(8,128)(2,1)S(1)}, u32[]{:S(2)}, u32[]{:S(2)}) collective-permute-start(bf16[256,3200]{1,0:T(8,128)(2,1)S(1)} %collective-permute-done.3), channel_id=1, source_target_pairs={{0,7},{1,0},{2,1},{3,2},{4,3},{5,4},{6,5},{7,6},{8,15},{9,8},{10,9... | collective-permute-start | bytes 4915208 | tf_op jit(solution)/shard_map/ppermute | solution.py:27
  124.2 20.4 %collective-permute-start.6 = (bf16[256,3200]{1,0:T(8,128)(2,1)S(1)}, bf16[256,3200]{1,0:T(8,128)(2,1)S(1)}, u32[]{:S(2)}, u32[]{:S(2)}) collective-permute-start(bf16[256,3200]{1,0:T(8,128)(2,1)S(1)} %collective-permute-done.4), channel_id=1, source_target_pairs={{0,1},{1,2},{2,3},{3,4},{4,5},{5,6},{6,7},{7,0},{8,9},{9,10},{10,1... | collective-permute-start | bytes 4915208 | tf_op jit(solution)/shard_map/ppermute | solution.py:22
  169.1 1.6 copy-start
  199.3 1.3 copy-start.5
  201.3 7.8 %copy-start.6 = (bf16[2048,2,128]{2,0,1:T(8,128)(2,1)S(1)}, bf16[2048,2,128]{2,0,1:T(8,128)(2,1)}, u32[]{:S(2)}) copy-start(bf16[2048,2,128]{2,0,1:T(8,128)(2,1)} %get-tuple-element.161) | copy-start | bytes 3145732 | tf_op jit(solution)/shard_map/while
  214.7 7.8 %copy-start.6 = (bf16[2048,2,128]{2,0,1:T(8,128)(2,1)S(1)}, bf16[2048,2,128]{2,0,1:T(8,128)(2,1)}, u32[]{:S(2)}) copy-start(bf16[2048,2,128]{2,0,1:T(8,128)(2,1)} %get-tuple-element.161) | copy-start | bytes 3145732 | tf_op jit(solution)/shard_map/while
  228.2 7.8 %copy-start.6 = (bf16[2048,2,128]{2,0,1:T(8,128)(2,1)S(1)}, bf16[2048,2,128]{2,0,1:T(8,128)(2,1)}, u32[]{:S(2)}) copy-start(bf16[2048,2,128]{2,0,1:T(8,128)(2,1)} %get-tuple-element.161) | copy-start | bytes 3145732 | tf_op jit(solution)/shard_map/while
  241.6 7.8 %copy-start.6 = (bf16[2048,2,128]{2,0,1:T(8,128)(2,1)S(1)}, bf16[2048,2,128]{2,0,1:T(8,128)(2,1)}, u32[]{:S(2)}) copy-start(bf16[2048,2,128]{2,0,1:T(8,128)(2,1)} %get-tuple-element.161) | copy-start | bytes 3145732 | tf_op jit(solution)/shard_map/while
  254.3 8.5 %copy-start.2 = (bf16[1,256,3200]{2,1,0:T(8,128)(2,1)S(1)}, bf16[1,256,3200]{2,1,0:T(8,128)(2,1)}, u32[]{:S(2)}) copy-start(bf16[1,256,3200]{2,1,0:T(8,128)(2,1)} %param.15) | copy-start | bytes 4915204
  255.8 22.1 %all-to-all-start = ((bf16[8,256,256]{2,1,0:T(8,128)(2,1)}), bf16[8,256,256]{2,1,0:T(8,128)(2,1)S(1)}, u32[]{:S(2)}, u32[]{:S(2)}) async-start(bf16[8,256,256]{2,1,0:T(8,128)(2,1)} %reshape_reshape.3), calls=%async_computation | async-start | bytes 2097152 | tf_op jit(solution)/shard_map/all_to_all | solution.py:123
  262.8 2.8 copy-start.7
  262.8 2.9 copy-start.8
  288.5 5.3 %copy-start.3 = (f32[4,2,16,2,3200]{4,3,2,1,0:T(2,128)S(1)}, f32[4,2,16,2,3200]{4,3,2,1,0:T(2,128)}, u32[]{:S(2)}) copy-start(f32[4,2,16,2,3200]{4,3,2,1,0:T(2,128)} %reshape.214) | copy-start | bytes 9830404
  288.5 5.3 %copy-start.11 = (f32[3200]{0:T(1024)S(1)}, f32[3200]{0:T(1024)}, u32[]{:S(2)}) copy-start(f32[3200]{0:T(1024)} %param.20) | copy-start | bytes 38404
  309.4 9.0 %copy-start.14 = (s32[1,256]{1,0:T(1,128)S(1)}, s32[1,256]{1,0:T(1,128)}, u32[]{:S(2)}) copy-start(s32[1,256]{1,0:T(1,128)} %param.22) | copy-start | bytes 3076
  309.4 10.0 %copy-start.15 = (s32[16]{0:T(128)S(1)}, s32[16]{0:T(128)}, u32[]{:S(2)}) copy-start(s32[16]{0:T(128)} %param.27) | copy-start | bytes 196
  309.4 31.5 %all-to-all-start.1 = ((bf16[64,16,800]{2,0,1:T(8,128)(2,1)}), bf16[64,16,800]{2,0,1:T(8,128)(2,1)S(1)}, u32[]{:S(2)}, u32[]{:S(2)}) async-start(bf16[64,16,800]{2,0,1:T(8,128)(2,1)} %copy.37), calls=%async_computation.1 | async-start | bytes 3670016 | tf_op jit(solution)/shard_map/all_to_all | solution.py:147
  317.8 138.7 %reduce-scatter.2.cloned.1.call-start = ((), (), s32[]{:S(2)}) async-start(), calls=%async_computation.3 | async-start | bytes 13369344 | tf_op jit(solution)/shard_map/reduce_scatter | solution.py:164
  361.4 95.2 %copy-start.9 = (f32[6144]{0:T(1024)S(1)}, f32[6144]{0:T(1024)}, u32[]{:S(2)}) copy-start(f32[6144]{0:T(1024)} %param.26) | copy-start | bytes 73732
Sparse Core Ops, SparseCore 0:
  18.4 93.5 all-gather.2
  361.5 94.9 reduce-scatter.1
